TPU v7x, 128 devices: a whole 4x4x4 slice. The times are simulated.
128 devices in a mesh: grp: 32 (over y, z, core), feat: 4 (over x).
Axes of the slice: x: 4, y: 4, z: 4, core: 2. Of those that a mesh axis runs over, the one named last changes fastest.
Arguments:
- hot_table: bfloat16 [16384, 1024], P(None, 'feat'), may hold values from -6 to 6
- cold_table: bfloat16 [131072, 1024], P('grp', 'feat'), may hold values from -6 to 6
- send_blocks: int32 [32, 32, 6], P('grp'), may hold values from 0 to 31
- block_counts: int32 [32, 32], P('grp'), may hold values from 1 to 6
- self_ref: int32 [90112], P('grp'), may hold values from 0 to 40959
- neigh_ref: int32 [90112, 10], P('grp'), may hold values from 0 to 40959
- route_owner: int32 [81920, 1], P('grp'), may hold values from 0 to 31; in each aligned block of 2560 rows (0 to 2559, 2560 to 5119, ...) at most 160 rows name the same one
- route_slot: int32 [81920], P('grp'), may hold values from 0 to 255
- w1_self: bfloat16 [1024, 512], P('feat'), may hold values from -0.1875 to 0.1875
- w1_neigh: bfloat16 [1024, 512], P('feat'), may hold values from -0.1875 to 0.1875
- b1_bias: float32 [512], P('feat'), may hold values from -3 to 3
- w2_self: bfloat16 [512, 512], P('feat'), may hold values from -0.25 to 0.25
- w2_neigh: bfloat16 [512, 512], P('feat'), may hold values from -0.25 to 0.25
- b2_bias: float32 [512], P('feat'), may hold values from -3 to 3
Outputs:
- embedding: bfloat16 [8192, 512], P('grp', 'feat')
Inputs may be any that keep to these rules, and one draw needn't show every extreme that they name: `route_owner`: in every draw some index of grp sends exactly 160 routed rows to one owner.
All inputs are finite; a program needn't handle non-finite values.
Results may differ from a plain program's by a relative error of at most 0.0047.
Values may be sent and summed in bfloat16 or wider, within the bound.
No kernel may reach another device: no remote copies, remote signals or barrier semaphores. Data moves between devices by JAX's collectives and lax.ppermute only.
A program may use at most 192 MiB of HBM per device.

v0:
```python
import jax
import jax.numpy as jnp
from jax import lax
from jax.sharding import PartitionSpec as P

BLK = 128
S1 = 10


def per_device(
    hot_table,
    cold_table,
    send_blocks,
    block_counts,
    self_ref,
    neigh_ref,
    route_owner,
    route_slot,
    w1_self,
    w1_neigh,
    b1_bias,
    w2_self,
    w2_neigh,
    b2_bias,
):
    groups = lax.axis_size("grp")
    feat_cols = cold_table.shape[1]
    slot_count = send_blocks.shape[2]
    cold_local = cold_table.reshape(-1, BLK, feat_cols)
    outgoing = cold_local[send_blocks[0]]
    valid = jnp.arange(slot_count, dtype=jnp.int32)[None, :] < block_counts[0][:, None]
    outgoing = jnp.where(valid[:, :, None, None], outgoing, jnp.zeros_like(outgoing))
    fetched = lax.all_to_all(outgoing, "grp", split_axis=0, concat_axis=0, tiled=True)
    cold_rows = fetched.reshape(-1, feat_cols)
    table = jnp.concatenate([hot_table, cold_rows], axis=0)
    self_x = table[self_ref]
    neigh_total = jnp.sum(table[neigh_ref], axis=1, dtype=jnp.float32)
    neigh_x = (neigh_total / S1).astype(jnp.bfloat16)
    hidden_cols = b1_bias.shape[0]
    partial_value = jnp.dot(self_x, w1_self, preferred_element_type=jnp.float32) + jnp.dot(
        neigh_x, w1_neigh, preferred_element_type=jnp.float32
    )
    summed = lax.psum(partial_value, "feat")
    pre = lax.dynamic_slice_in_dim(summed, lax.axis_index("feat") * hidden_cols, hidden_cols, 1)
    h1 = jnp.maximum(pre + b1_bias, 0.0).astype(jnp.bfloat16)
    targets = h1.shape[0] - route_slot.shape[0]
    own_rows = h1[:targets]
    routed = h1[targets:]
    owner = route_owner[:, 0]
    capacity = 2 * routed.shape[0] // groups
    onehot_owner = (owner[:, None] == jnp.arange(groups, dtype=jnp.int32)[None, :]).astype(
        jnp.int32
    )
    position = jnp.sum((jnp.cumsum(onehot_owner, axis=0) - 1) * onehot_owner, axis=1)
    place = owner * capacity + position
    send_rows = jnp.zeros((groups * capacity, hidden_cols), jnp.bfloat16).at[place].set(routed)
    send_slots = jnp.full((groups * capacity,), -1, jnp.int32).at[place].set(route_slot)
    recv_rows, recv_slots = (
        lax.all_to_all(
            send_rows.reshape(groups, capacity, hidden_cols),
            "grp",
            split_axis=0,
            concat_axis=0,
            tiled=True,
        ),
        lax.all_to_all(
            send_slots.reshape(groups, capacity), "grp", split_axis=0, concat_axis=0, tiled=True
        ),
    )
    recv_rows = recv_rows.reshape(groups * capacity, hidden_cols)
    recv_slots = recv_slots.reshape(groups * capacity)
    member = jnp.arange(targets, dtype=jnp.int32)[:, None] == recv_slots[None, :]
    total = jnp.dot(member.astype(jnp.bfloat16), recv_rows, preferred_element_type=jnp.float32)
    count = jnp.sum(member.astype(jnp.float32), axis=1)
    neigh_h = (total / jnp.maximum(count, 1.0)[:, None]).astype(jnp.bfloat16)
    partial_two = jnp.dot(own_rows, w2_self, preferred_element_type=jnp.float32) + jnp.dot(
        neigh_h, w2_neigh, preferred_element_type=jnp.float32
    )
    shared = lax.psum_scatter(partial_two, "feat", scatter_dimension=1, tiled=True)
    return (shared + b2_bias).astype(jnp.bfloat16)


def solution(mesh):
    in_specs = (
        P(None, "feat"),
        P("grp", "feat"),
        P("grp", None, None),
        P("grp", None),
        P("grp"),
        P("grp", None),
        P("grp", None),
        P("grp"),
        P("feat", None),
        P("feat", None),
        P("feat"),
        P("feat", None),
        P("feat", None),
        P("feat"),
    )
    out_specs = P("grp", "feat")
    return jax.shard_map(
        per_device, mesh=mesh, in_specs=in_specs, out_specs=out_specs, check_vma=False
    )
```

profile of v0, /device:TPU:0, one launch (start us, length us, event | category | flops | bytes accessed | tf_op | source)
XLA Modules:
  0.0 589.9 jit_solution(16499131093047876776)
XLA Ops:
  6.5 0.8 compare_select_fusion.3
  7.6 0.7 iota_compare_fusion.10
  8.3 8.1 %gather_fusion = bf16[192,128,256]{2,1,0:T(8,128)(2,1)} fusion(bf16[32,128,256]{2,1,0:T(8,128)(2,1)S(1)} %bitcast.33, s32[1024]{0:T(1024)S(1)} %pad_clamp_fusion.2), kind=kCustom, calls=%fused_computation | custom fusion | bytes 25166592 | tf_op jit(solution)/shard_map/gather | solution.py:30
  16.5 10.6 %broadcast_select_fusion = bf16[32,6,128,256]{3,2,1,0:T(8,128)(2,1)} fusion(bf16[32,6,128,256]{3,2,1,0:T(8,128)(2,1)} %bitcast.34, pred[32,6]{1,0:T(8,128)(4,1)S(1)} %iota_compare_fusion.10), kind=kLoop, calls=%fused_computation.6 | loop fusion | flops 6291456 | bytes 25166016 | tf_op jit(solution)/shard_map/jit(_where)/select_n | solution.py:32
  27.1 8.7 %all-to-all-start = ((bf16[32,6,128,256]{3,2,1,0:T(8,128)(2,1)}), bf16[32,6,128,256]{3,2,1,0:T(8,128)(2,1)}, u32[]{:S(2)}, u32[]{:S(2)}) async-start(bf16[32,6,128,256]{3,2,1,0:T(8,128)(2,1)} %broadcast_select_fusion), calls=%async_computation | async-start | bytes 25165824 | tf_op jit(solution)/shard_map/all_to_all | solution.py:33
  35.9 0.5 copy.20
  36.4 1.1 reshape.117
  37.5 175.6 %all-to-all-done = bf16[32,6,128,256]{3,2,1,0:T(8,128)(2,1)} async-done(((bf16[32,6,128,256]{3,2,1,0:T(8,128)(2,1)}), bf16[32,6,128,256]{3,2,1,0:T(8,128)(2,1)}, u32[]{:S(2)}, u32[]{:S(2)}) %all-to-all-start) | async-done | bytes 12582944 | tf_op jit(solution)/shard_map/all_to_all | solution.py:33
  213.1 21.5 %pad_maximum_fusion = bf16[40960,256]{1,0:T(8,128)(2,1)} fusion(bf16[24576,256]{1,0:T(8,128)(2,1)} %bitcast.4, bf16[16384,256]{1,0:T(8,128)(2,1)} %param.14), kind=kLoop, calls=%fused_computation.5 | loop fusion | flops 41943040 | bytes 41943040 | tf_op jit(solution)/shard_map/concatenate | solution.py:35
  234.6 15.9 %gather_fusion.1 = bf16[2816,256]{1,0:T(8,128)(2,1)S(1)} fusion(bf16[40960,256]{1,0:T(8,128)(2,1)} %pad_maximum_fusion, s32[3072]{0:T(1024)S(1)} %pad_clamp_fusion.1), kind=kCustom, calls=%fused_computation.1 | custom fusion | bytes 2894848 | tf_op jit(solution)/shard_map/gather | solution.py:36
  250.5 73.4 %gather_fusion.2 = bf16[28160,256]{1,0:T(8,128)(2,1)} fusion(bf16[40960,256]{1,0:T(8,128)(2,1)} %pad_maximum_fusion, s32[28672]{0:T(1024)S(1)} %pad_clamp_fusion), kind=kCustom, calls=%fused_computation.2 | custom fusion | bytes 28948480 | tf_op jit(solution)/shard_map/gather | solution.py:37
  323.9 28.8 %reshape.143 = f32[2816,10,256]{2,1,0:T(8,128)} reshape(bf16[28160,256]{1,0:T(8,128)(2,1)} %gather_fusion.2) | data formatting | bytes 43253760 | tf_op jit(solution)/shard_map/convert_element_type | solution.py:37
  352.8 3.4 fusion.18
  356.1 22.0 %reduce_sum.29 = f32[2816,256]{1,0:T(8,128)} reduce(f32[2816,10,256]{2,1,0:T(8,128)} %reshape.143, f32[]{:T(128)} %constant.17.clone.1), dimensions={1}, to_apply=%region_0.1 | reduce | flops 6488064 | bytes 31719428 | tf_op jit(solution)/shard_map/reduce_sum | solution.py:37
  378.1 6.9 %convolution_add_fusion = f32[2816,512]{1,0:T(8,128)} fusion(f32[2816,512]{1,0:T(8,128)} %fusion.18, bf16[256,512]{1,0:T(8,128)(2,1)S(1)} %copy-done.2, f32[2816,256]{1,0:T(8,128)} %reduce_sum.29), kind=kOutput, calls=%fused_computation.10 | convolution fusion | flops 741081088 | bytes 14680064 | tf_op jit(solution)/shard_map/dot_general | solution.py:40
  385.0 0.7 copy-done.6
  385.8 9.4 %reduce-window.6 = s32[32,20,128]{2,1,0:T(8,128)S(1)} reduce-window(s32[32,20,128]{2,1,0:T(8,128)S(1)} %fusion.8, s32[]{:T(128)} %constant.13.clone.1), window={size=1x1x128 pad=0_0x0_0x127_0}, to_apply=%region_2.3 | reduce-window | flops 10403840 | bytes 655364 | tf_op jit(solution)/shard_map/reduce-window
  395.3 0.3 copy.23
  395.8 0.2 add_add_fusion
  396.1 10.1 %scatter_custom_fusion = s32[5120]{0:T(1024)S(1)} fusion(s32[2560]{0:T(1024)S(1)} %fusion.14, s32[2560]{0:T(1024)} %param.21, s32[]{:T(128)} %constant.22.clone.1), kind=kCustom, calls=%fused_computation.40 | custom fusion | bytes 20992 | tf_op jit(solution)/shard_map/scatter | solution.py:57
  406.2 0.7 all_to_all.13
  407.0 25.3 %all-to-all-start.1 = ((s32[32,1,160]{2,1,0:T(1,128)}), s32[32,1,160]{2,1,0:T(1,128)S(1)}, u32[]{:S(2)}, u32[]{:S(2)}) async-start(s32[32,1,160]{2,1,0:T(1,128)} %all_to_all.13), calls=%async_computation.1 | async-start | bytes 65536 | tf_op jit(solution)/shard_map/all_to_all | solution.py:66
  432.3 90.5 %all-reduce.2.cloned.1.call-done = f32[2816,512]{1,0:T(8,128)} async-done(((f32[2816,512]{1,0:T(8,128)}), f32[2816,512]{1,0:T(8,128)}) %all-reduce.2.cloned.1.call-update) | async-done | bytes 5767184 | tf_op jit(solution)/shard_map/psum | solution.py:43
  522.9 1.7 maximum_convert_fusion
  524.5 8.2 %scatter_custom_fusion.1 = bf16[5120,128]{1,0:T(8,128)(2,1)} fusion(s32[2560]{0:T(1024)S(1)} %fusion.14, bf16[2816,128]{1,0:T(8,128)(2,1)S(1)} %maximum_convert_fusion, bf16[]{:T(256)} %constant.15.clone.1), kind=kCustom, calls=%fused_computation.18 | custom fusion | bytes 1966082 | tf_op jit(solution)/shard_map/scatter | solution.py:56
  532.8 7.4 %all-to-all-start.2 = ((bf16[32,160,128]{2,1,0:T(8,128)(2,1)}), bf16[32,160,128]{2,1,0:T(8,128)(2,1)}, u32[]{:S(2)}, u32[]{:S(2)}) async-start(bf16[32,160,128]{2,1,0:T(8,128)(2,1)} %bitcast.8), calls=%async_computation.2 | async-start | bytes 2621440 | tf_op jit(solution)/shard_map/all_to_all | solution.py:59
  540.4 0.6 convert_reduce_fusion
  541.0 0.2 fusion.11
  541.2 18.7 %all-to-all-done.2 = bf16[32,160,128]{2,1,0:T(8,128)(2,1)} async-done(((bf16[32,160,128]{2,1,0:T(8,128)(2,1)}), bf16[32,160,128]{2,1,0:T(8,128)(2,1)}, u32[]{:S(2)}, u32[]{:S(2)}) %all-to-all-start.2) | async-done | bytes 1310752 | tf_op jit(solution)/shard_map/all_to_all | solution.py:59
  559.9 3.3 convolution_add_fusion.1
  563.2 18.3 %reduce-scatter.2.cloned.1.call-done = f32[256,128]{1,0:T(8,128)} async-done(((f32[256,512]{1,0:T(8,128)}), f32[256,128]{1,0:T(8,128)}) %reduce-scatter.2.cloned.1.call-update) | async-done | bytes 131088 | tf_op jit(solution)/shard_map/reduce_scatter | solution.py:79
  581.5 1.5 add_convert_fusion
  (40 shorter events, 1.1 us)
Async XLA Ops:
  6.5 1.8 copy-start
  27.1 8.8 %copy-start.4 = (s32[2816,10]{0,1:T(8,128)S(1)}, s32[2816,10]{0,1:T(8,128)}, u32[]{:S(2)}) copy-start(s32[2816,10]{0,1:T(8,128)} %param.19) | copy-start | bytes 337924
  27.1 10.4 %copy-start.7 = (s32[2816]{0:T(1024)S(1)}, s32[2816]{0:T(1024)}, u32[]{:S(2)}) copy-start(s32[2816]{0:T(1024)} %param.18) | copy-start | bytes 33796
  27.1 186.0 %all-to-all-start = ((bf16[32,6,128,256]{3,2,1,0:T(8,128)(2,1)}), bf16[32,6,128,256]{3,2,1,0:T(8,128)(2,1)}, u32[]{:S(2)}, u32[]{:S(2)}) async-start(bf16[32,6,128,256]{3,2,1,0:T(8,128)(2,1)} %broadcast_select_fusion), calls=%async_computation | async-start | bytes 25165824 | tf_op jit(solution)/shard_map/all_to_all | solution.py:33
  35.8 487.1 %all-reduce.2.cloned.1.call-start = ((), (), s32[]{:S(2)}) async-start(), calls=%async_computation.4 | async-start | bytes 11534336 | tf_op jit(solution)/shard_map/psum | solution.py:43
  323.9 28.8 %copy-start.3 = (bf16[256,512]{1,0:T(8,128)(2,1)S(1)}, bf16[256,512]{1,0:T(8,128)(2,1)}, u32[]{:S(2)}) copy-start(bf16[256,512]{1,0:T(8,128)(2,1)} %param.22) | copy-start | bytes 786436
  356.1 22.0 %copy-start.2 = (bf16[256,512]{1,0:T(8,128)(2,1)S(1)}, bf16[256,512]{1,0:T(8,128)(2,1)}, u32[]{:S(2)}) copy-start(bf16[256,512]{1,0:T(8,128)(2,1)} %param.23) | copy-start | bytes 786436
  385.0 0.7 copy-start.6
  385.0 137.9 %copy-start.9 = (f32[128]{0:T(128)S(1)}, f32[128]{0:T(128)}, u32[]{:S(2)}) copy-start(f32[128]{0:T(128)} %param.24) | copy-start | bytes 1540
  385.8 155.2 %copy-start.5 = (bf16[128,512]{1,0:T(8,128)(2,1)S(1)}, bf16[128,512]{1,0:T(8,128)(2,1)}, u32[]{:S(2)}) copy-start(bf16[128,512]{1,0:T(8,128)(2,1)} %param.25) | copy-start | bytes 393220
  407.0 125.8 %all-to-all-start.1 = ((s32[32,1,160]{2,1,0:T(1,128)}), s32[32,1,160]{2,1,0:T(1,128)S(1)}, u32[]{:S(2)}, u32[]{:S(2)}) async-start(s32[32,1,160]{2,1,0:T(1,128)} %all_to_all.13), calls=%async_computation.1 | async-start | bytes 65536 | tf_op jit(solution)/shard_map/all_to_all | solution.py:66
  522.9 60.2 %copy-start.1 = (bf16[4096,256]{1,0:T(8,128)(2,1)S(1)}, bf16[4096,256]{1,0:T(8,128)(2,1)}, u32[]{:S(2)}) copy-start(bf16[4096,256]{1,0:T(8,128)(2,1)} %param.15) | copy-start | bytes 6291460
  524.5 57.0 %copy-start.8 = (f32[128]{0:T(128)S(1)}, f32[128]{0:T(128)}, u32[]{:S(2)}) copy-start(f32[128]{0:T(128)} %param.27) | copy-start | bytes 1540
  532.8 27.2 %all-to-all-start.2 = ((bf16[32,160,128]{2,1,0:T(8,128)(2,1)}), bf16[32,160,128]{2,1,0:T(8,128)(2,1)}, u32[]{:S(2)}, u32[]{:S(2)}) async-start(bf16[32,160,128]{2,1,0:T(8,128)(2,1)} %bitcast.8), calls=%async_computation.2 | async-start | bytes 2621440 | tf_op jit(solution)/shard_map/all_to_all | solution.py:59
  540.2 41.4 %reduce-scatter.2.cloned.1.call-start = ((), (), s32[]{:S(2)}) async-start(), calls=%async_computation.5 | async-start | bytes 655360 | tf_op jit(solution)/shard_map/reduce_scatter | solution.py:79
Sparse Core Ops, SparseCore 0:
  385.2 137.6 all-reduce.1
  563.3 18.1 reduce-scatter.1
where the time goes:
time: 592 us; the launch traced here: 590 us
  waiting for transfers between devices  303 us (51%)
  local copies, waits for them, and re-layouts  148 us (25%)
  other arithmetic  69.5 us (12%)
  starting transfers between devices  41.5 us (7%)
  matrix products  13.7 us (2%)
  between operations  13.6 us (2%)
    all_to_all x1, waiting for transfers between devices, per_device(): lax.all_to_all(outgoing, 'grp', split_axis=0, concat_axis=0, tiled=True)  176 us
    psum x1, waiting for transfers between devices, per_device(): summed = lax.psum(partial_value, 'feat')  90.5 us
    gather x1, local copies, waits for them, and re-layouts, per_device(): neigh_total = jnp.sum(table[neigh_ref], axis=1, dtype=jnp.float32)  73.4 us
    convert_element_type x1, local copies, waits for them, and re-layouts, per_device(): neigh_total = jnp.sum(table[neigh_ref], axis=1, dtype=jnp.float32)  28.8 us
    all_to_all x1, starting transfers between devices, per_device(): lax.all_to_all(send_slots.reshape(groups, capacity), 'grp', split_axis=0,...  25.3 us
    reduce_sum x1, other arithmetic, per_device(): neigh_total = jnp.sum(table[neigh_ref], axis=1, dtype=jnp.float32)  22 us
    concatenate x1, other arithmetic, per_device(): table = jnp.concatenate([hot_table, cold_rows], axis=0)  21.5 us
    all_to_all x1, waiting for transfers between devices, per_device(): lax.all_to_all(send_rows.reshape(groups, capacity, hidden_cols), 'grp', s...  18.7 us
  transfers between devices with their start and end apart: 5, of which 4 were waited for; matrix products, arithmetic and copies ran while one was open for 6% of the time, Pallas kernels for 0%

commit v1 on v0

--- a/solution.py
+++ b/solution.py
@@ -40,7 +40,9 @@
     partial_value = jnp.dot(self_x, w1_self, preferred_element_type=jnp.float32) + jnp.dot(
         neigh_x, w1_neigh, preferred_element_type=jnp.float32
     )
-    summed = lax.psum(partial_value, "feat")
+    summed = partial_value
+    for hop in (1, 2):
+        summed = summed + lax.ppermute(summed, "feat", [(dev, dev ^ hop) for dev in range(4)])
     pre = lax.dynamic_slice_in_dim(summed, lax.axis_index("feat") * hidden_cols, hidden_cols, 1)
     h1 = jnp.maximum(pre + b1_bias, 0.0).astype(jnp.bfloat16)
     targets = h1.shape[0] - route_slot.shape[0]

time: 592 us -> 729 us (1.23)
  waiting for transfers between devices: 303 us -> 406 us
  starting transfers between devices: 41.5 us -> 74.6 us
    ppermute x0 -> x2, waiting for transfers between devices: none -> 191 us  [per_device(): lax.ppermute(summed, 'feat', [(dev, dev ^ hop) for dev in range(4)])]
    psum x1 -> x0, waiting for transfers between devices: 90.5 us -> none  [per_device(): summed = lax.psum(partial_value, 'feat')]
    all_to_all x1, starting transfers between devices: 7.38 us -> 32.2 us  [per_device(): lax.all_to_all(send_rows.reshape(groups, capacity, hidden_cols), 'grp', s...]
  transfers between devices with their start and end apart: 5 -> 6, of which waited for: 4 -> 5; matrix products, arithmetic and copies ran while one was open for 6% -> 5% of each run, Pallas kernels for 0% -> 0%
where the time goes in v1:
time: 729 us; the launch traced here: 727 us
  waiting for transfers between devices  406 us (56%)
  local copies, waits for them, and re-layouts  148 us (20%)
  starting transfers between devices  74.6 us (10%)
  other arithmetic  73.9 us (10%)
  between operations  13.6 us (2%)
  matrix products  11.2 us (2%)
    ppermute x2, waiting for transfers between devices, per_device(): lax.ppermute(summed, 'feat', [(dev, dev ^ hop) for dev in range(4)])  191 us
    all_to_all x1, waiting for transfers between devices, per_device(): lax.all_to_all(outgoing, 'grp', split_axis=0, concat_axis=0, tiled=True)  176 us
    gather x1, local copies, waits for them, and re-layouts, per_device(): neigh_total = jnp.sum(table[neigh_ref], axis=1, dtype=jnp.float32)  73.4 us
    all_to_all x1, starting transfers between devices, per_device(): lax.all_to_all(send_rows.reshape(groups, capacity, hidden_cols), 'grp', s...  32.2 us
    all_to_all x1, starting transfers between devices, per_device(): lax.all_to_all(send_slots.reshape(groups, capacity), 'grp', split_axis=0,...  28.9 us
    convert_element_type x1, local copies, waits for them, and re-layouts, per_device(): neigh_total = jnp.sum(table[neigh_ref], axis=1, dtype=jnp.float32)  28.8 us
    reduce_sum x1, other arithmetic, per_device(): neigh_total = jnp.sum(table[neigh_ref], axis=1, dtype=jnp.float32)  22.2 us
    concatenate x1, other arithmetic, per_device(): table = jnp.concatenate([hot_table, cold_rows], axis=0)  21.5 us
  transfers between devices with their start and end apart: 6, of which 5 were waited for; matrix products, arithmetic and copies ran while one was open for 5% of the time, Pallas kernels for 0%

profile of v1, /device:TPU:0, one launch (start us, length us, event | category | flops | bytes accessed | tf_op | source)
XLA Modules:
  0.0 726.8 jit_solution(11752288568135953567)
XLA Ops:
  6.5 0.8 compare_select_fusion.3
  7.6 0.7 iota_compare_fusion.10
  8.3 8.1 %gather_fusion = bf16[192,128,256]{2,1,0:T(8,128)(2,1)} fusion(bf16[32,128,256]{2,1,0:T(8,128)(2,1)S(1)} %bitcast.33, s32[1024]{0:T(1024)S(1)} %pad_clamp_fusion.2), kind=kCustom, calls=%fused_computation | custom fusion | bytes 25166592 | tf_op jit(solution)/shard_map/gather | solution.py:30
  16.5 10.6 %broadcast_select_fusion = bf16[32,6,128,256]{3,2,1,0:T(8,128)(2,1)} fusion(bf16[32,6,128,256]{3,2,1,0:T(8,128)(2,1)} %bitcast.34, pred[32,6]{1,0:T(8,128)(4,1)S(1)} %iota_compare_fusion.10), kind=kLoop, calls=%fused_computation.6 | loop fusion | flops 6291456 | bytes 25166016 | tf_op jit(solution)/shard_map/jit(_where)/select_n | solution.py:32
  27.1 8.9 %all-to-all-start = ((bf16[32,6,128,256]{3,2,1,0:T(8,128)(2,1)}), bf16[32,6,128,256]{3,2,1,0:T(8,128)(2,1)}, u32[]{:S(2)}, u32[]{:S(2)}) async-start(bf16[32,6,128,256]{3,2,1,0:T(8,128)(2,1)} %broadcast_select_fusion), calls=%async_computation | async-start | bytes 25165824 | tf_op jit(solution)/shard_map/all_to_all | solution.py:33
  36.5 1.1 reshape.117
  37.7 175.5 %all-to-all-done = bf16[32,6,128,256]{3,2,1,0:T(8,128)(2,1)} async-done(((bf16[32,6,128,256]{3,2,1,0:T(8,128)(2,1)}), bf16[32,6,128,256]{3,2,1,0:T(8,128)(2,1)}, u32[]{:S(2)}, u32[]{:S(2)}) %all-to-all-start) | async-done | bytes 12582944 | tf_op jit(solution)/shard_map/all_to_all | solution.py:33
  213.2 21.5 %pad_maximum_fusion = bf16[40960,256]{1,0:T(8,128)(2,1)} fusion(bf16[24576,256]{1,0:T(8,128)(2,1)} %bitcast.4, bf16[16384,256]{1,0:T(8,128)(2,1)} %param.14), kind=kLoop, calls=%fused_computation.5 | loop fusion | flops 41943040 | bytes 41943040 | tf_op jit(solution)/shard_map/concatenate | solution.py:35
  234.7 15.9 %gather_fusion.1 = bf16[2816,256]{1,0:T(8,128)(2,1)S(1)} fusion(bf16[40960,256]{1,0:T(8,128)(2,1)} %pad_maximum_fusion, s32[3072]{0:T(1024)S(1)} %pad_clamp_fusion.1), kind=kCustom, calls=%fused_computation.1 | custom fusion | bytes 2894848 | tf_op jit(solution)/shard_map/gather | solution.py:36
  250.6 73.4 %gather_fusion.2 = bf16[28160,256]{1,0:T(8,128)(2,1)} fusion(bf16[40960,256]{1,0:T(8,128)(2,1)} %pad_maximum_fusion, s32[28672]{0:T(1024)S(1)} %pad_clamp_fusion), kind=kCustom, calls=%fused_computation.2 | custom fusion | bytes 28948480 | tf_op jit(solution)/shard_map/gather | solution.py:37
  324.0 28.8 %reshape.143 = f32[2816,10,256]{2,1,0:T(8,128)} reshape(bf16[28160,256]{1,0:T(8,128)(2,1)} %gather_fusion.2) | data formatting | bytes 43253760 | tf_op jit(solution)/shard_map/convert_element_type | solution.py:37
  352.9 3.4 fusion.21
  356.2 22.2 %reduce_sum.29 = f32[2816,256]{1,0:T(8,128)} reduce(f32[2816,10,256]{2,1,0:T(8,128)} %reshape.143, f32[]{:T(128)} %constant.17.clone.1), dimensions={1}, to_apply=%region_0.1 | reduce | flops 6488064 | bytes 31719428 | tf_op jit(solution)/shard_map/reduce_sum | solution.py:37
  378.4 4.4 convolution_add_fusion
  382.9 1.6 collective-permute-start
  384.5 121.0 %collective-permute-done = f32[2816,512]{1,0:T(8,128)S(1)} collective-permute-done((f32[2816,512]{1,0:T(8,128)S(1)}, f32[2816,512]{1,0:T(8,128)S(1)}, u32[]{:S(2)}, u32[]{:S(2)}) %collective-permute-start) | collective-permute-done | bytes 5767200 | tf_op jit(solution)/shard_map/ppermute | solution.py:45
  505.5 3.9 add.77
  509.4 3.0 collective-permute-start.1
  512.5 9.2 %reduce-window.6 = s32[32,20,128]{2,1,0:T(8,128)S(1)} reduce-window(s32[32,20,128]{2,1,0:T(8,128)S(1)} %fusion.12, s32[]{:T(128)} %constant.13.clone.1), window={size=1x1x128 pad=0_0x0_0x127_0}, to_apply=%region_1.2 | reduce-window | flops 10403840 | bytes 655364 | tf_op jit(solution)/shard_map/reduce-window
  522.6 10.1 %scatter_custom_fusion = s32[5120]{0:T(1024)S(1)} fusion(s32[2560]{0:T(1024)S(1)} %fusion.17, s32[2560]{0:T(1024)} %param.21, s32[]{:T(128)} %constant.22.clone.1), kind=kCustom, calls=%fused_computation.43 | custom fusion | bytes 20992 | tf_op jit(solution)/shard_map/scatter | solution.py:59
  532.7 0.7 all_to_all.13
  533.5 28.9 %all-to-all-start.1 = ((s32[32,1,160]{2,1,0:T(1,128)}), s32[32,1,160]{2,1,0:T(1,128)S(1)}, u32[]{:S(2)}, u32[]{:S(2)}) async-start(s32[32,1,160]{2,1,0:T(1,128)} %all_to_all.13), calls=%async_computation.1 | async-start | bytes 65536 | tf_op jit(solution)/shard_map/all_to_all | solution.py:68
  562.4 70.5 %collective-permute-done.1 = f32[2816,512]{1,0:T(8,128)} collective-permute-done((f32[2816,512]{1,0:T(8,128)}, f32[2816,512]{1,0:T(8,128)}, u32[]{:S(2)}, u32[]{:S(2)}) %collective-permute-start.1) | collective-permute-done | bytes 5767200 | tf_op jit(solution)/shard_map/ppermute | solution.py:45
  632.9 2.2 fusion.4
  635.0 8.2 %scatter_custom_fusion.1 = bf16[5120,128]{1,0:T(8,128)(2,1)} fusion(s32[2560]{0:T(1024)S(1)} %fusion.17, bf16[2816,128]{1,0:T(8,128)(2,1)S(1)} %fusion.4, bf16[]{:T(256)} %constant.15.clone.1), kind=kCustom, calls=%fused_computation.22 | custom fusion | bytes 1966082 | tf_op jit(solution)/shard_map/scatter | solution.py:58
  643.3 32.2 %all-to-all-start.2 = ((bf16[32,160,128]{2,1,0:T(8,128)(2,1)}), bf16[32,160,128]{2,1,0:T(8,128)(2,1)}, u32[]{:S(2)}, u32[]{:S(2)}) async-start(bf16[32,160,128]{2,1,0:T(8,128)(2,1)} %bitcast.8), calls=%async_computation.2 | async-start | bytes 2621440 | tf_op jit(solution)/shard_map/all_to_all | solution.py:61
  675.7 0.6 convert_reduce_fusion
  676.3 18.9 %all-to-all-done.2 = bf16[32,160,128]{2,1,0:T(8,128)(2,1)} async-done(((bf16[32,160,128]{2,1,0:T(8,128)(2,1)}), bf16[32,160,128]{2,1,0:T(8,128)(2,1)}, u32[]{:S(2)}, u32[]{:S(2)}) %all-to-all-start.2) | async-done | bytes 1310752 | tf_op jit(solution)/shard_map/all_to_all | solution.py:61
  695.3 2.4 fusion.8
  697.7 1.0 convolution_add_fusion.1
  698.7 19.7 %reduce-scatter.2.cloned.1.call-done = f32[256,128]{1,0:T(8,128)} async-done(((f32[256,512]{1,0:T(8,128)}), f32[256,128]{1,0:T(8,128)}) %reduce-scatter.2.cloned.1.call-update) | async-done | bytes 131088 | tf_op jit(solution)/shard_map/reduce_scatter | solution.py:81
  718.4 1.5 add_convert_fusion
  (42 shorter events, 2.0 us)
Async XLA Ops:
  6.5 1.8 copy-start
  27.1 8.9 %copy-start.4 = (s32[2816,10]{0,1:T(8,128)S(1)}, s32[2816,10]{0,1:T(8,128)}, u32[]{:S(2)}) copy-start(s32[2816,10]{0,1:T(8,128)} %param.19) | copy-start | bytes 337924
  27.1 10.5 %copy-start.7 = (s32[2816]{0:T(1024)S(1)}, s32[2816]{0:T(1024)}, u32[]{:S(2)}) copy-start(s32[2816]{0:T(1024)} %param.18) | copy-start | bytes 33796
  27.1 186.1 %all-to-all-start = ((bf16[32,6,128,256]{3,2,1,0:T(8,128)(2,1)}), bf16[32,6,128,256]{3,2,1,0:T(8,128)(2,1)}, u32[]{:S(2)}, u32[]{:S(2)}) async-start(bf16[32,6,128,256]{3,2,1,0:T(8,128)(2,1)} %broadcast_select_fusion), calls=%async_computation | async-start | bytes 25165824 | tf_op jit(solution)/shard_map/all_to_all | solution.py:33
  324.0 28.8 %copy-start.3 = (bf16[256,512]{1,0:T(8,128)(2,1)S(1)}, bf16[256,512]{1,0:T(8,128)(2,1)}, u32[]{:S(2)}) copy-start(bf16[256,512]{1,0:T(8,128)(2,1)} %param.22) | copy-start | bytes 786436
  356.2 22.2 %copy-start.2 = (bf16[256,512]{1,0:T(8,128)(2,1)S(1)}, bf16[256,512]{1,0:T(8,128)(2,1)}, u32[]{:S(2)}) copy-start(bf16[256,512]{1,0:T(8,128)(2,1)} %param.23) | copy-start | bytes 786436
  382.9 129.5 %copy-start.6 = (s32[2560,1]{0,1:T(1,128)S(1)}, s32[2560,1]{0,1:T(1,128)}, u32[]{:S(2)}) copy-start(s32[2560,1]{0,1:T(1,128)} %param.20) | copy-start | bytes 30724
  382.9 250.0 %copy-start.8 = (f32[128]{0:T(128)S(1)}, f32[128]{0:T(128)}, u32[]{:S(2)}) copy-start(f32[128]{0:T(128)} %param.24) | copy-start | bytes 1540
  382.9 122.6 %collective-permute-start = (f32[2816,512]{1,0:T(8,128)S(1)}, f32[2816,512]{1,0:T(8,128)S(1)}, u32[]{:S(2)}, u32[]{:S(2)}) collective-permute-start(f32[2816,512]{1,0:T(8,128)S(1)} %convolution_add_fusion), channel_id=1, source_target_pairs={{0,1},{1,0},{2,3},{3,2},{4,5},{5,4},{6,7},{7,6},{8,9},{9,8},{10,11... | collective-permute-start | bytes 17301512 | tf_op jit(solution)/shard_map/ppermute | solution.py:45
  509.4 123.5 %collective-permute-start.1 = (f32[2816,512]{1,0:T(8,128)}, f32[2816,512]{1,0:T(8,128)}, u32[]{:S(2)}, u32[]{:S(2)}) collective-permute-start(f32[2816,512]{1,0:T(8,128)} %add.77), channel_id=1, source_target_pairs={{0,2},{1,3},{2,0},{3,1},{4,6},{5,7},{6,4},{7,5},{8,10},{9,11},{10,... | collective-permute-start | bytes 17301512 | tf_op jit(solution)/shard_map/ppermute | solution.py:45
  533.5 109.8 %all-to-all-start.1 = ((s32[32,1,160]{2,1,0:T(1,128)}), s32[32,1,160]{2,1,0:T(1,128)S(1)}, u32[]{:S(2)}, u32[]{:S(2)}) async-start(s32[32,1,160]{2,1,0:T(1,128)} %all_to_all.13), calls=%async_computation.1 | async-start | bytes 65536 | tf_op jit(solution)/shard_map/all_to_all | solution.py:68
  562.4 135.3 %copy-start.5 = (bf16[128,512]{1,0:T(8,128)(2,1)S(1)}, bf16[128,512]{1,0:T(8,128)(2,1)}, u32[]{:S(2)}) copy-start(bf16[128,512]{1,0:T(8,128)(2,1)} %param.25) | copy-start | bytes 393220
  632.9 87.1 %copy-start.1 = (bf16[4096,256]{1,0:T(8,128)(2,1)S(1)}, bf16[4096,256]{1,0:T(8,128)(2,1)}, u32[]{:S(2)}) copy-start(bf16[4096,256]{1,0:T(8,128)(2,1)} %param.15) | copy-start | bytes 6291460
  635.0 83.4 %copy-start.9 = (f32[128]{0:T(128)S(1)}, f32[128]{0:T(128)}, u32[]{:S(2)}) copy-start(f32[128]{0:T(128)} %param.27) | copy-start | bytes 1540
  643.3 52.0 %all-to-all-start.2 = ((bf16[32,160,128]{2,1,0:T(8,128)(2,1)}), bf16[32,160,128]{2,1,0:T(8,128)(2,1)}, u32[]{:S(2)}, u32[]{:S(2)}) async-start(bf16[32,160,128]{2,1,0:T(8,128)(2,1)} %bitcast.8), calls=%async_computation.2 | async-start | bytes 2621440 | tf_op jit(solution)/shard_map/all_to_all | solution.py:61
  675.5 42.9 %reduce-scatter.2.cloned.1.call-start = ((), (), s32[]{:S(2)}) async-start(), calls=%async_computation.4 | async-start | bytes 655360 | tf_op jit(solution)/shard_map/reduce_scatter | solution.py:81
Sparse Core Ops, SparseCore 0:
  698.9 19.5 reduce-scatter.1
